TPU v7x, 128 devices: a whole 4x4x4 slice. The times are simulated.
128 devices in a mesh: ctx: 32 (over y, z, core), fsdp: 4 (over x).
Axes of the slice: x: 4, y: 4, z: 4, core: 2. Of those that a mesh axis runs over, the one named last changes fastest.
Arguments:
- gate_in: bfloat16 [16384, 4096], P('ctx', 'fsdp'), may hold values from -6 to 6
- values: bfloat16 [16384, 4096], P('ctx', 'fsdp'), may hold values from -6 to 6
- gate_out: bfloat16 [16384, 4096], P('ctx', 'fsdp'), may hold values from -6 to 6
- bias: float32 [4096], P('fsdp'), may hold values from -4 to 4
- spectrum: bfloat16 [2, 32768, 4096], P(None, ('ctx', 'fsdp')), may hold values from -6 to 6
Outputs:
- gated: bfloat16 [16384, 4096], P('ctx', 'fsdp')
All inputs are finite; a program needn't handle non-finite values.
Results may differ from a plain program's by a relative error of at most 0.0049.
Values may be sent and summed in bfloat16 or wider, within the bound.
No kernel may reach another device: no remote copies, remote signals or barrier semaphores. Data moves between devices by JAX's collectives and lax.ppermute only.
A program may use at most 128 MiB of HBM per device.

v0:
```python
import functools
import math

import jax
import jax.numpy as jnp
from jax import lax
from jax.experimental import pallas as pl
from jax.experimental.pallas import tpu as pltpu
from jax.sharding import PartitionSpec as P


LANES = 512
RADIX = 4
SPREAD = 1.624475


def cosine(step, modulus):
    half = modulus // 2
    centred = jnp.bitwise_and(step + half, modulus - 1) - half
    y = (modulus // 4 - jnp.abs(centred)).astype(jnp.float32) * (2.0 * math.pi / modulus)
    z = y * y
    series = 1.0 / 6227020800.0
    for term in (-1.0 / 39916800.0, 1.0 / 362880.0, -1.0 / 5040.0, 1.0 / 120.0, -1.0 / 6.0, 1.0):
        series = series * z + term
    return series * y


def message(index, block):
    fine = block // RADIX
    return index % fine * RADIX + index // (2 * fine) % RADIX, index // fine % 2


def cross_table(devices, block, transpose):
    wide = jnp.arange(2 * devices * block, dtype=jnp.int32)
    residue = wide // (2 * block)
    wide_row, part = message(wide, block)
    narrow = jnp.arange(devices * block, dtype=jnp.int32)
    place, narrow_row = narrow // block, narrow % block
    first = residue == 0
    rate = jnp.where(first, part * devices, residue)
    phase = jnp.where(first, 0, part * (devices // 2))
    if transpose:
        step = place[:, None] * rate[None, :] + phase[None, :]
        same = narrow_row[:, None] == wide_row[None, :]
    else:
        step = rate[:, None] * place[None, :] + phase[:, None]
        same = wide_row[:, None] == narrow_row[None, :]
    return jnp.where(same, cosine(step, 2 * devices) * SPREAD, 0.0).astype(jnp.bfloat16)


def local_table(position, devices, rows, block, transpose):
    length = 2 * devices * rows
    stride = 2 * devices
    fine = block // RADIX
    quart = rows // RADIX
    first = position == 0
    out = jnp.arange(4 * quart, dtype=jnp.int32)
    group, out_part, order = out // (2 * quart), out // quart % 2, out % quart
    rate = jnp.where(first, stride * order + group * devices, stride * (order + 2 * quart * group) + position)
    inp = jnp.arange(2 * devices * fine, dtype=jnp.int32)
    in_part = inp // fine % 2
    base = inp // (2 * fine) * block + inp % fine * RADIX
    in_phase = jnp.where(first, 0, in_part)
    side = jnp.where(first, group, 2)
    digit = jnp.arange(RADIX, dtype=jnp.int32)[:, None, None]
    quarter = length // 4
    if transpose:
        row = digit + base[None, :, None]
        step = row * rate[None, None, :] + quarter * (out_part[None, None, :] - in_phase[None, :, None])
        keep = (side[None, :] == 2) | (side[None, :] == in_part[:, None])
    else:
        row = digit + base[None, None, :]
        step = row * rate[None, :, None] + quarter * (out_part[None, :, None] - in_phase[None, None, :])
        keep = (side[:, None] == 2) | (side[:, None] == in_part[None, :])
    return jnp.where(keep[None], cosine(step, length), 0.0).astype(jnp.bfloat16)


def each_block(width, step):
    def go(i, carry):
        step(i, pl.ds(pl.multiple_of(i * LANES, LANES), LANES))
        return carry

    lax.fori_loop(0, width // LANES, go, 0)


def cross_kernel(scale, table_ref, x_ref, o_hbm, o_buf, o_sem):
    def store(i, cols):
        return pltpu.make_async_copy(o_buf.at[:, cols], o_hbm.at[:, cols], o_sem.at[i])

    def step(i, cols):
        acc = jnp.dot(table_ref[...], x_ref[:, cols], preferred_element_type=jnp.float32)
        o_buf[:, cols] = (acc * scale).astype(o_buf.dtype)
        store(i, cols).start()

    each_block(x_ref.shape[1], step)
    each_block(x_ref.shape[1], lambda i, cols: store(i, cols).wait())


def fold_kernel(scale, table_ref, x_ref, o_ref):
    def step(i, cols):
        acc = jnp.dot(table_ref[...], x_ref[:, cols], preferred_element_type=jnp.float32)
        o_ref[:, cols] = (acc * scale).astype(o_ref.dtype)

    each_block(x_ref.shape[1], step)


def local_kernel(
    m_hbm, g_hbm, own_hbm, near_hbm, far_hbm, last_hbm, x_hbm, o_hbm,
    m_ref, g_ref, r_ref, x_ref, o_ref, b_ref, m_sem, g_sem, r_sem, x_sem, o_sem,
):
    quart, width = r_ref.shape[2] // 2, r_ref.shape[3]
    first = lax.axis_index("ctx") == 0
    member = lax.axis_index("fsdp")
    members = r_ref.shape[0]

    forward = pltpu.make_async_copy(m_hbm, m_ref, m_sem)
    backward = pltpu.make_async_copy(g_hbm, g_ref, g_sem)

    def filters(i, cols):
        mine = pl.ds(pl.multiple_of(member * width + i * LANES, LANES), LANES)
        sources = [own_hbm.at[:, :, mine]] + [piece.at[:, :, cols] for piece in (near_hbm, far_hbm, last_hbm)]
        return [
            pltpu.make_async_copy(source, r_ref.at[shift, :, :, cols], r_sem.at[shift, i])
            for shift, source in enumerate(sources)
        ]

    def response(group, cols):
        here = jnp.where(first, 2 * group, group)
        there = jnp.where(first, 2 * group + 1, members - 1 - group)
        here = lax.rem(member + members - here, members)
        there = lax.rem(member + members - there, members)
        size = 2 * quart
        row = lax.broadcasted_iota(jnp.int32, (size, size), 0)
        col = lax.broadcasted_iota(jnp.int32, (size, size), 1)
        shifted = jnp.where(first, 1, 0) if group == 0 else 0
        mirror = jnp.where(row + col == size - 1 + shifted, 0.5, 0.0).astype(jnp.bfloat16)
        even = 0.5 * r_ref[here, 0, :, cols].astype(jnp.float32) + jnp.dot(
            mirror, r_ref[there, 0, :, cols], preferred_element_type=jnp.float32
        )
        odd = 0.5 * r_ref[here, 1, :, cols].astype(jnp.float32) - jnp.dot(
            mirror, r_ref[there, 1, :, cols], preferred_element_type=jnp.float32
        )
        return even, odd, there

    def incoming(i, cols):
        return pltpu.make_async_copy(x_hbm.at[:, :, :, cols], x_ref.at[:, :, :, cols], x_sem.at[i])

    def store(i, cols):
        return pltpu.make_async_copy(o_ref.at[:, :, :, cols], o_hbm.at[:, :, :, cols], o_sem.at[i])

    def start(copies):
        for copy in copies:
            copy.start()

    def wait(copies):
        for copy in copies:
            copy.wait()

    forward.start()
    for i in range(width // LANES):
        incoming(i, pl.ds(i * LANES, LANES)).start()
        start(filters(i, pl.ds(i * LANES, LANES)))
    backward.start()
    forward.wait()

    def ahead(i, cols):
        incoming(i, cols).wait()
        v = []
        for digit in range(RADIX):
            x = x_ref[:, digit, :, cols]
            x = x.reshape(-1, x.shape[-1])
            v.append(jnp.dot(m_ref[digit], x, preferred_element_type=jnp.float32))
        wait(filters(i, cols))
        sum02, sum13, gap02, gap13 = v[0] + v[2], v[1] + v[3], v[0] - v[2], v[1] - v[3]
        total = sum02 + sum13
        for group in range(2):
            even, odd, there = response(group, cols)
            if group == 0:
                lone = first & (lax.broadcasted_iota(jnp.int32, (8, LANES), 0) == 0)
                edge = jnp.where(lone, 0.5 * r_ref[there, 0, :8, cols].astype(jnp.float32), 0.0)
                edge = (sum02[:8] - sum13[:8]) * edge
            at = 2 * group * quart
            re, im = slice(at, at + quart), slice(at + quart, at + 2 * quart)
            parts = []
            for turn, (real, imag) in enumerate(
                ((total[re], total[im]), (gap02[re] + gap13[im], gap02[im] - gap13[re]))
            ):
                here = slice(turn * quart, (turn + 1) * quart)
                parts.append((real * even[here] - imag * odd[here], real * odd[here] + imag * even[here]))
            (r0, i0), (r1, i1) = parts
            for digit, (real, imag) in enumerate(
                ((r0 + r1, i0 + i1), (r0 - i1, i0 + r1), (r0 - r1, i0 - i1), (r0 + i1, i0 - r1))
            ):
                if group == 0:
                    top = real[:8] + edge if digit % 2 == 0 else real[:8] - edge
                    real = jnp.concatenate([top, real[8:]], axis=0)
                b_ref[digit, re, cols] = real.astype(b_ref.dtype)
                b_ref[digit, im, cols] = imag.astype(b_ref.dtype)

    def back(i, cols):
        for digit in range(RADIX):
            y = jnp.dot(g_ref[digit], b_ref[digit, :, cols], preferred_element_type=jnp.float32)
            o_ref[:, digit, :, cols] = y.reshape(o_ref.shape[0], o_ref.shape[2], -1).astype(o_ref.dtype)
        store(i, cols).start()

    each_block(width, ahead)
    backward.wait()
    each_block(width, back)
    each_block(width, lambda i, cols: store(i, cols).wait())


def gate_kernel(restored_ref, mixed_ref, gate_ref, bias_ref, o_hbm, o_buf, o_sem):
    rows = o_buf.shape[0] // o_sem.shape[0]
    bias = bias_ref[...]

    def store(i):
        at = pl.ds(i * rows, rows)
        return pltpu.make_async_copy(o_buf.at[at], o_hbm.at[at], o_sem.at[i])

    for i in range(o_sem.shape[0]):
        at = slice(i * rows, (i + 1) * rows)
        convolved = restored_ref[at].astype(jnp.float32) + bias * mixed_ref[at].astype(jnp.float32)
        o_buf[at] = (gate_ref[at].astype(jnp.float32) * convolved).astype(o_buf.dtype)
        store(i).start()
    for i in range(o_sem.shape[0]):
        store(i).wait()


def call(kernel, stored, near, out, scratch, grant):
    there = pl.BlockSpec(memory_space=pltpu.HBM)
    return pl.pallas_call(
        kernel,
        in_specs=[there] * len(stored) + [pl.BlockSpec(memory_space=pltpu.VMEM)] * len(near),
        out_specs=jax.tree.map(lambda _: there, out),
        out_shape=out,
        scratch_shapes=scratch,
        compiler_params=pltpu.CompilerParams(vmem_limit_bytes=grant << 20),
    )(*stored, *near)


def apply_cross(table, x, scale):
    out = jax.ShapeDtypeStruct((table.shape[0], x.shape[1]), jnp.bfloat16)
    scratch = [pltpu.VMEM(out.shape, out.dtype), pltpu.SemaphoreType.DMA((x.shape[1] // LANES,))]
    return call(functools.partial(cross_kernel, scale), (), (table, x), out, scratch, 12)


def apply_fold(table, x, scale):
    vmem = pl.BlockSpec(memory_space=pltpu.VMEM)
    return pl.pallas_call(
        functools.partial(fold_kernel, scale),
        in_specs=[vmem] * 2,
        out_specs=vmem,
        out_shape=jax.ShapeDtypeStruct((table.shape[0], x.shape[1]), jnp.bfloat16),
        name="fold",
        compiler_params=pltpu.CompilerParams(vmem_limit_bytes=12 << 20),
    )(table, x)


def apply_local(forward, backward, pieces, x):
    count = x.shape[-1] // LANES
    rows = forward.shape[1]
    dma = pltpu.SemaphoreType.DMA
    stored = pltpu.VMEM((len(pieces), *pieces[1].shape), x.dtype)
    scratch = [pltpu.VMEM(forward.shape, x.dtype), pltpu.VMEM(backward.shape, x.dtype), stored]
    scratch += [pltpu.VMEM(x.shape, x.dtype), pltpu.VMEM(x.shape, x.dtype)]
    scratch += [pltpu.VMEM((RADIX, rows, x.shape[-1]), x.dtype)]
    scratch += [dma(()), dma(()), dma((len(pieces), count)), dma((count,)), dma((count,))]
    out = jax.ShapeDtypeStruct(x.shape, x.dtype)
    return call(local_kernel, (forward, backward, *pieces, x), (), out, scratch, 62)


def mix_kernel(left_hbm, right_hbm, stored_hbm, o_hbm, far_hbm, left, right, o_buf, in_sem, far_sem, o_sem):
    blocks = o_sem.shape[0]
    rows = o_buf.shape[0] // blocks
    width = far_hbm.shape[2]
    target = lax.rem(lax.axis_index("fsdp") + 2, stored_hbm.shape[2] // width)

    def loads(i):
        at = pl.ds(i * rows, rows)
        return [
            pltpu.make_async_copy(left_hbm.at[at], left.at[at], in_sem.at[0, i]),
            pltpu.make_async_copy(right_hbm.at[at], right.at[at], in_sem.at[1, i]),
        ]

    def store(i):
        at = pl.ds(i * rows, rows)
        return pltpu.make_async_copy(o_buf.at[at], o_hbm.at[at], o_sem.at[i])

    for i in range(blocks):
        for load in loads(i):
            load.start()
    mine = pl.ds(pl.multiple_of(target * width, width), width)
    far = pltpu.make_async_copy(stored_hbm.at[:, :, mine], far_hbm, far_sem)
    far.start()
    for i in range(blocks):
        for load in loads(i):
            load.wait()
        at = slice(i * rows, (i + 1) * rows)
        o_buf[at] = (left[at].astype(jnp.float32) * right[at].astype(jnp.float32)).astype(o_buf.dtype)
        store(i).start()
    for i in range(blocks):
        store(i).wait()
    far.wait()


def apply_mix(left, right, stored):
    dma = pltpu.SemaphoreType.DMA
    scratch = [pltpu.VMEM(left.shape, left.dtype)] * 3 + [dma((2, 4)), dma(()), dma((4,))]
    piece = jax.ShapeDtypeStruct((*stored.shape[:2], left.shape[1]), stored.dtype)
    out = (jax.ShapeDtypeStruct(left.shape, left.dtype), piece)
    return call(mix_kernel, (left, right, stored), (), out, scratch, 62)


def apply_gate(restored, mixed, gate_out, bias):
    scratch = [pltpu.VMEM(mixed.shape, mixed.dtype), pltpu.SemaphoreType.DMA((4,))]
    out = jax.ShapeDtypeStruct(mixed.shape, mixed.dtype)
    return call(gate_kernel, (), (restored, mixed, gate_out, bias[None, :]), out, scratch, 8)


def exchange(array):
    return lax.all_to_all(array, "ctx", split_axis=0, concat_axis=0, tiled=True)


def body(gate_in, values, gate_out, bias, spectrum):
    devices = lax.axis_size("ctx")
    members = lax.axis_size("fsdp")
    rows, channels = gate_in.shape
    block = rows // devices
    length = 2 * rows * devices
    position = lax.axis_index("ctx")
    member = lax.axis_index("fsdp")

    def piece_for(stored, shift):
        target = lax.rem(member + shift, members)
        return lax.dynamic_slice_in_dim(stored, target * channels, channels, 2)

    def send(piece, shift):
        return lax.ppermute(piece, "fsdp", [(m, (m + shift) % members) for m in range(members)])

    mixed, far = apply_mix(gate_in, values, spectrum)
    mixed, far, later = lax.optimization_barrier((mixed, far, spectrum))
    stage = exchange(mixed.reshape(devices, block, channels))
    far = send(far, 2)
    near, last = piece_for(later, 1), piece_for(later, members - 1)
    pieces = (spectrum, send(near, 1), far, send(last, members - 1))

    cross = cross_table(devices, block, False)
    cross_back = cross_table(devices, block, True)
    local = local_table(position, devices, rows, block, False)
    local_back = local_table(position, devices, rows, block, True)

    spread = apply_cross(cross, stage.reshape(rows, channels), 1.0 / SPREAD)
    stage = exchange(spread.reshape(devices, 2 * block, channels))
    turned = apply_local(local, local_back, pieces, stage.reshape(devices, RADIX, -1, channels))
    stage = exchange(turned.reshape(devices, 2 * block, channels))
    folded = apply_fold(cross_back, stage.reshape(2 * rows, channels), 2.0 / (length * SPREAD))
    restored = exchange(folded.reshape(devices, block, channels)).reshape(rows, channels)
    return apply_gate(restored, mixed, gate_out, bias)


def solution(mesh):
    return jax.shard_map(
        body,
        mesh=mesh,
        in_specs=(
            P("ctx", "fsdp"),
            P("ctx", "fsdp"),
            P("ctx", "fsdp"),
            P("fsdp"),
            P(None, ("ctx", "fsdp"), None),
        ),
        out_specs=P("ctx", "fsdp"),
        check_vma=False,
    )
```

profile of v0, /device:TPU:1, one launch (start us, length us, event | category | flops | bytes accessed | tf_op | source)
XLA Modules:
  0.0 167.6 jit_solution(16035256969198426675)
XLA Ops:
  0.0 33.0 %shard_map.55 = (bf16[512,1024]{1,0:T(8,128)(2,1)}, bf16[2,256,1024]{2,1,0:T(8,128)(2,1)}) custom-call(bf16[512,1024]{1,0:T(8,128)(2,1)} %left_hbm.1, bf16[512,1024]{1,0:T(8,128)(2,1)} %right_hbm.1, bf16[2,256,4096]{2,1,0:T(8,128)(2,1)} %own_hbm.1), custom_call_target="tpu_custom_call" | custom-call | tf_op jit(solution)/shard_map/pallas_call | solution.py:231
  33.0 2.8 %constant_dynamic-slice_fusion = (bf16[2,256,1024]{2,1,0:T(8,128)(2,1)S(1)}, bf16[2,256,1024]{2,1,0:T(8,128)(2,1)}) fusion(bf16[2,256,4096]{2,1,0:T(8,128)(2,1)} %own_hbm.1, s32[]{:T(128)S(6)} %select_n.443, s32[]{:T(128)S(6)} %select_n.442), kind=kLoop, calls=%fused_computation.126 | loop fusion | bytes 4194312 | tf_op jit(solution)/shard_map/dynamic_slice | solution.py:335
  35.8 2.0 %collective-permute-start = (bf16[2,256,1024]{2,1,0:T(8,128)(2,1)}, bf16[2,256,1024]{2,1,0:T(8,128)(2,1)}, u32[]{:S(2)}, u32[]{:S(2)}) collective-permute-start(bf16[2,256,1024]{2,1,0:T(8,128)(2,1)} %get-tuple-element.16), channel_id=1, source_target_pairs={{0,1},{1,2},{2,3},{3,0},{4,5},{5,6},{6,7},{7,4},{8,9},{9,10},{10,1... | collective-permute-start | bytes 3145736 | tf_op jit(solution)/shard_map/ppermute | solution.py:338
  37.8 1.3 collective-permute-start.2
  39.1 9.5 %all-to-all-start = ((bf16[32,16,1024]{2,1,0:T(8,128)(2,1)}), bf16[32,16,1024]{2,1,0:T(8,128)(2,1)S(1)}, u32[]{:S(2)}, u32[]{:S(2)}) async-start(bf16[32,16,1024]{2,1,0:T(8,128)(2,1)} %bitcast), calls=%async_computation | async-start | bytes 2097152 | tf_op jit(solution)/shard_map/all_to_all | solution.py:321
  48.6 1.6 collective-permute-start.1
  50.3 0.2 compare_or_fusion
  50.5 2.3 %select_convert_fusion.table_ref = bf16[1024,512]{1,0:T(8,128)(2,1)S(1)} fusion(s32[1024]{0:T(1024)S(1)} %get-tuple-element.17, s32[512]{0:T(512)S(1)} %get-tuple-element.19, s32[1024]{0:T(1024)S(1)} %get-tuple-element.18, s32[512]{0:T(512)S(1)} %get-tuple-element.20, s32[1024]{0:T(1024)S(1)} %fusion.23), kind=kLoop, calls=%fused_computation | loop fusion | flops 14155776 | bytes 1064960 | tf_op jit(solution)/shard_map/convert_element_type | solution.py:48
  52.8 12.7 %all-to-all-done = bf16[32,16,1024]{2,1,0:T(8,128)(2,1)S(1)} async-done(((bf16[32,16,1024]{2,1,0:T(8,128)(2,1)}), bf16[32,16,1024]{2,1,0:T(8,128)(2,1)S(1)}, u32[]{:S(2)}, u32[]{:S(2)}) %all-to-all-start) | async-done | bytes 1048608 | tf_op jit(solution)/shard_map/all_to_all | solution.py:321
  65.5 2.5 %shard_map.56 = bf16[1024,1024]{1,0:T(8,128)(2,1)} custom-call(bf16[1024,512]{1,0:T(8,128)(2,1)S(1)} %select_convert_fusion.table_ref, bf16[512,1024]{1,0:T(8,128)(2,1)S(1)} %bitcast.11), custom_call_target="tpu_custom_call" | custom-call | tf_op jit(solution)/shard_map/pallas_call | solution.py:231
  68.0 4.6 %all-to-all-start.1 = ((bf16[32,32,1024]{2,1,0:T(8,128)(2,1)}), bf16[32,32,1024]{2,1,0:T(8,128)(2,1)}, u32[]{:S(2)}, u32[]{:S(2)}) async-start(bf16[32,32,1024]{2,1,0:T(8,128)(2,1)} %bitcast.2), calls=%async_computation.1 | async-start | bytes 4194304 | tf_op jit(solution)/shard_map/all_to_all | solution.py:321
  72.6 0.2 compare_or_fusion.1
  72.8 0.1 subtract_multiply_fusion
  72.9 0.1 subtract_multiply_fusion.1
  73.1 2.9 %select_convert_fusion.2.m_hbm = bf16[4,512,256]{2,1,0:T(8,128)(2,1)} fusion(s32[512,256]{1,0:T(8,128)S(1)} %subtract_multiply_fusion.1, s32[512]{0:T(512)S(1)} %fusion.37, s32[4,256]{1,0:T(4,128)S(1)} %iota_add_fusion, pred[512,256]{1,0:T(8,128)(4,1)S(1)} %compare_or_fusion.1), kind=kLoop, calls=%fused_computation.18 | loop fusion | flops 13107200 | bytes 1710080 | tf_op jit(solution)/shard_map/convert_element_type | solution.py:75
  76.0 2.8 %select_convert_fusion.1.g_hbm = bf16[4,256,512]{2,1,0:T(8,128)(2,1)} fusion(s32[256,512]{1,0:T(8,128)S(1)} %subtract_multiply_fusion, s32[512]{0:T(512)S(1)} %fusion.37, s32[4,256]{1,0:T(4,128)S(1)} %iota_add_fusion, pred[256,512]{1,0:T(8,128)(4,1)S(1)} %compare_or_fusion), kind=kLoop, calls=%fused_computation.9 | loop fusion | flops 13107200 | bytes 1710080 | tf_op jit(solution)/shard_map/convert_element_type | solution.py:75
  78.8 0.0 collective-permute-done.near_hbm
  78.8 0.0 collective-permute-done.2.last_hbm
  78.8 6.8 %collective-permute-done.1.far_hbm = bf16[2,256,1024]{2,1,0:T(8,128)(2,1)} collective-permute-done((bf16[2,256,1024]{2,1,0:T(8,128)(2,1)}, bf16[2,256,1024]{2,1,0:T(8,128)(2,1)}, u32[]{:S(2)}, u32[]{:S(2)}) %collective-permute-start.1) | collective-permute-done | bytes 1048608 | tf_op jit(solution)/shard_map/ppermute | solution.py:338
  85.6 15.3 %all-to-all-done.1 = bf16[32,32,1024]{2,1,0:T(8,128)(2,1)} async-done(((bf16[32,32,1024]{2,1,0:T(8,128)(2,1)}), bf16[32,32,1024]{2,1,0:T(8,128)(2,1)}, u32[]{:S(2)}, u32[]{:S(2)}) %all-to-all-start.1) | async-done | bytes 2097184 | tf_op jit(solution)/shard_map/all_to_all | solution.py:321
  101.0 9.1 %shard_map.57 = bf16[32,4,8,1024]{3,2,1,0:T(8,128)(2,1)} custom-call(bf16[4,512,256]{2,1,0:T(8,128)(2,1)} %select_convert_fusion.2.m_hbm, bf16[4,256,512]{2,1,0:T(8,128)(2,1)} %select_convert_fusion.1.g_hbm, bf16[2,256,4096]{2,1,0:T(8,128)(2,1)} %own_hbm.1, bf16[2,256,1024]{2,1,0:T(8,128)(2,1)} %collective-permute-done.near_hbm, ...), custom_call_target="tpu_custom_call" | custom-call | tf_op jit(solution)/shard_map/pallas_call | solution.py:231
  110.1 4.5 %all-to-all-start.2 = ((bf16[32,32,1024]{2,1,0:T(8,128)(2,1)}), bf16[32,32,1024]{2,1,0:T(8,128)(2,1)S(1)}, u32[]{:S(2)}, u32[]{:S(2)}) async-start(bf16[32,32,1024]{2,1,0:T(8,128)(2,1)} %bitcast.14), calls=%async_computation.2 | async-start | bytes 4194304 | tf_op jit(solution)/shard_map/all_to_all | solution.py:321
  114.6 2.5 %select_convert_fusion.3.table_ref = bf16[512,1024]{1,0:T(8,128)(2,1)S(1)} fusion(s32[1024]{0:T(1024)S(1)} %get-tuple-element.17, s32[1024]{0:T(1024)S(1)} %get-tuple-element.18, s32[512]{0:T(512)S(1)} %get-tuple-element.19, s32[1024]{0:T(1024)S(1)} %fusion.23, s32[512]{0:T(512)S(1)} %get-tuple-element.20), kind=kLoop, calls=%fused_computation.27 | loop fusion | flops 14155776 | bytes 1064960 | tf_op jit(solution)/shard_map/convert_element_type | solution.py:48
  117.1 25.9 %all-to-all-done.2 = bf16[32,32,1024]{2,1,0:T(8,128)(2,1)S(1)} async-done(((bf16[32,32,1024]{2,1,0:T(8,128)(2,1)}), bf16[32,32,1024]{2,1,0:T(8,128)(2,1)S(1)}, u32[]{:S(2)}, u32[]{:S(2)}) %all-to-all-start.2) | async-done | bytes 2097184 | tf_op jit(solution)/shard_map/all_to_all | solution.py:321
  143.0 1.4 fold.1
  144.5 0.0 copy-start
  144.5 0.0 copy-start.1
  144.5 20.6 %all_to_all.20 = bf16[32,16,1024]{2,1,0:T(8,128)(2,1)S(1)} all-to-all(bf16[32,16,1024]{2,1,0:T(8,128)(2,1)S(1)} %bitcast.12), channel_id=1, replica_groups=mesh['ctx'=32,'fsdp'=4] {'ctx'}, dimensions={0} | all-to-all | bytes 2097152 | tf_op jit(solution)/shard_map/all_to_all | solution.py:321
  165.1 0.0 copy-done
  165.1 0.0 copy-done.1
  165.1 2.4 %shard_map.58 = bf16[512,1024]{1,0:T(8,128)(2,1)} custom-call(bf16[512,1024]{1,0:T(8,128)(2,1)S(1)} %bitcast.10, bf16[512,1024]{1,0:T(8,128)(2,1)} %get-tuple-element.14.mixed_ref, bf16[512,1024]{1,0:T(8,128)(2,1)S(1)} %copy-done, f32[1,1024]{1,0:T(1,128)S(1)} %bitcast.13), custom_call_target="tpu_custom_call" | custom-call | tf_op jit(solution)/shard_map/pallas_call | solution.py:231
  (11 shorter events, 0.1 us)
Async XLA Ops:
  35.8 43.0 %collective-permute-start = (bf16[2,256,1024]{2,1,0:T(8,128)(2,1)}, bf16[2,256,1024]{2,1,0:T(8,128)(2,1)}, u32[]{:S(2)}, u32[]{:S(2)}) collective-permute-start(bf16[2,256,1024]{2,1,0:T(8,128)(2,1)} %get-tuple-element.16), channel_id=1, source_target_pairs={{0,1},{1,2},{2,3},{3,0},{4,5},{5,6},{6,7},{7,4},{8,9},{9,10},{10,1... | collective-permute-start | bytes 3145736 | tf_op jit(solution)/shard_map/ppermute | solution.py:338
  37.8 41.0 %collective-permute-start.2 = (bf16[2,256,1024]{2,1,0:T(8,128)(2,1)S(1)}, bf16[2,256,1024]{2,1,0:T(8,128)(2,1)}, u32[]{:S(2)}, u32[]{:S(2)}) collective-permute-start(bf16[2,256,1024]{2,1,0:T(8,128)(2,1)S(1)} %get-tuple-element.15), channel_id=1, source_target_pairs={{0,3},{1,0},{2,1},{3,2},{4,7},{5,4},{6,5},{7,6},{8,11},{9,8},{10,9... | collective-permute-start | bytes 3145736 | tf_op jit(solution)/shard_map/ppermute | solution.py:338
  39.1 26.4 %all-to-all-start = ((bf16[32,16,1024]{2,1,0:T(8,128)(2,1)}), bf16[32,16,1024]{2,1,0:T(8,128)(2,1)S(1)}, u32[]{:S(2)}, u32[]{:S(2)}) async-start(bf16[32,16,1024]{2,1,0:T(8,128)(2,1)} %bitcast), calls=%async_computation | async-start | bytes 2097152 | tf_op jit(solution)/shard_map/all_to_all | solution.py:321
  48.6 37.0 %collective-permute-start.1 = (bf16[2,256,1024]{2,1,0:T(8,128)(2,1)}, bf16[2,256,1024]{2,1,0:T(8,128)(2,1)}, u32[]{:S(2)}, u32[]{:S(2)}) collective-permute-start(bf16[2,256,1024]{2,1,0:T(8,128)(2,1)} %get-tuple-element.13), channel_id=1, source_target_pairs={{0,2},{1,3},{2,0},{3,1},{4,6},{5,7},{6,4},{7,5},{8,10},{9,11},{10,... | collective-permute-start | bytes 3145736 | tf_op jit(solution)/shard_map/ppermute | solution.py:338
  68.0 32.9 %all-to-all-start.1 = ((bf16[32,32,1024]{2,1,0:T(8,128)(2,1)}), bf16[32,32,1024]{2,1,0:T(8,128)(2,1)}, u32[]{:S(2)}, u32[]{:S(2)}) async-start(bf16[32,32,1024]{2,1,0:T(8,128)(2,1)} %bitcast.2), calls=%async_computation.1 | async-start | bytes 4194304 | tf_op jit(solution)/shard_map/all_to_all | solution.py:321
  110.1 32.9 %all-to-all-start.2 = ((bf16[32,32,1024]{2,1,0:T(8,128)(2,1)}), bf16[32,32,1024]{2,1,0:T(8,128)(2,1)S(1)}, u32[]{:S(2)}, u32[]{:S(2)}) async-start(bf16[32,32,1024]{2,1,0:T(8,128)(2,1)} %bitcast.14), calls=%async_computation.2 | async-start | bytes 4194304 | tf_op jit(solution)/shard_map/all_to_all | solution.py:321
  144.5 20.7 %copy-start = (bf16[512,1024]{1,0:T(8,128)(2,1)S(1)}, bf16[512,1024]{1,0:T(8,128)(2,1)}, u32[]{:S(2)}) copy-start(bf16[512,1024]{1,0:T(8,128)(2,1)} %gate_ref.1) | copy-start | bytes 3145732
  144.5 20.7 %copy-start.1 = (f32[1024]{0:T(1024)S(1)}, f32[1024]{0:T(1024)}, u32[]{:S(2)}) copy-start(f32[1024]{0:T(1024)} %param.8) | copy-start | bytes 12292
where the time goes:
time: 168 us
  waiting for transfers between devices  60.8 us (36%)
  Pallas kernels  48.4 us (29%)
  starting transfers between devices  23.5 us (14%)
  blocking collectives  20.6 us (12%)
  other arithmetic  11.2 us (7%)
  local copies, waits for them, and re-layouts  2.81 us (2%)
    all_to_all x3, waiting for transfers between devices, exchange(): return lax.all_to_all(array, 'ctx', split_axis=0, concat_axis=0, tiled=True)  54 us
    pallas_call x4, Pallas kernels, call(): pl.pallas_call(kernel, in_specs=[there] * len(stored) + [pl.BlockSpec(mem...  47 us
    all_to_all x1, blocking collectives, exchange(): return lax.all_to_all(array, 'ctx', split_axis=0, concat_axis=0, tiled=True)  20.6 us
    all_to_all x3, starting transfers between devices, exchange(): return lax.all_to_all(array, 'ctx', split_axis=0, concat_axis=0, tiled=True)  18.6 us
    ppermute x3, waiting for transfers between devices, send(): lax.ppermute(piece, 'fsdp', [(m, (m + shift) % members) for m in range(me...  6.81 us
    convert_element_type x2, other arithmetic, local_table(): return jnp.where(keep[None], cosine(step, length), 0.0).astype(jnp.bfloat16)  5.73 us
    ppermute x3, starting transfers between devices, send(): lax.ppermute(piece, 'fsdp', [(m, (m + shift) % members) for m in range(me...  4.91 us
    convert_element_type x2, other arithmetic, cross_table(): jnp.where(same, cosine(step, 2 * devices) * SPREAD, 0.0)  4.83 us
  transfers between devices with their start and end apart: 6, of which 4 were waited for; matrix products, arithmetic and copies ran while one was open for 7% of the time, Pallas kernels for 1%

commit v1 on v0

--- a/solution.py
+++ b/solution.py
@@ -269,7 +269,9 @@
     return call(local_kernel, (forward, backward, *pieces, x), (), out, scratch, 62)
 
 
-def mix_kernel(left_hbm, right_hbm, stored_hbm, o_hbm, far_hbm, left, right, o_buf, in_sem, far_sem, o_sem):
+def mix_kernel(
+    left_hbm, right_hbm, stored_hbm, o_hbm, far_hbm, left, right, o_buf, far_buf, in_sem, far_sem, o_sem
+):
     blocks = o_sem.shape[0]
     rows = o_buf.shape[0] // blocks
     width = far_hbm.shape[2]
@@ -290,23 +292,31 @@
         for load in loads(i):
             load.start()
     mine = pl.ds(pl.multiple_of(target * width, width), width)
-    far = pltpu.make_async_copy(stored_hbm.at[:, :, mine], far_hbm, far_sem)
-    far.start()
+    parts = range(far_buf.shape[0])
+    taken = [pltpu.make_async_copy(stored_hbm.at[p, :, mine], far_buf.at[p], far_sem.at[0, p]) for p in parts]
+    given = [pltpu.make_async_copy(far_buf.at[p], far_hbm.at[p], far_sem.at[1, p]) for p in parts]
+    for copy in taken:
+        copy.start()
     for i in range(blocks):
         for load in loads(i):
             load.wait()
         at = slice(i * rows, (i + 1) * rows)
         o_buf[at] = (left[at].astype(jnp.float32) * right[at].astype(jnp.float32)).astype(o_buf.dtype)
         store(i).start()
+    for p in parts:
+        taken[p].wait()
+        given[p].start()
     for i in range(blocks):
         store(i).wait()
-    far.wait()
+    for copy in given:
+        copy.wait()
 
 
 def apply_mix(left, right, stored):
     dma = pltpu.SemaphoreType.DMA
-    scratch = [pltpu.VMEM(left.shape, left.dtype)] * 3 + [dma((2, 4)), dma(()), dma((4,))]
     piece = jax.ShapeDtypeStruct((*stored.shape[:2], left.shape[1]), stored.dtype)
+    scratch = [pltpu.VMEM(left.shape, left.dtype)] * 3 + [pltpu.VMEM(piece.shape, piece.dtype)]
+    scratch += [dma((2, 4)), dma((2, piece.shape[0])), dma((4,))]
     out = (jax.ShapeDtypeStruct(left.shape, left.dtype), piece)
     return call(mix_kernel, (left, right, stored), (), out, scratch, 62)
 

time: 168 us -> 138 us (0.82)
  Pallas kernels: 48.4 us -> 18.2 us
    pallas_call x4, Pallas kernels: 47 us -> 16.8 us  [call(): pl.pallas_call(kernel, in_specs=[there] * len(stored) + [pl.BlockSpec(mem...]
  transfers between devices with their start and end apart: 6 -> 6, of which waited for: 4 -> 4; matrix products, arithmetic and copies ran while one was open for 7% -> 8% of each run, Pallas kernels for 1% -> 2%
where the time goes in v1:
time: 138 us; the launch traced here: 137 us
  waiting for transfers between devices  60.8 us (44%)
  starting transfers between devices  23.5 us (17%)
  blocking collectives  20.6 us (15%)
  Pallas kernels  18.2 us (13%)
  other arithmetic  11.2 us (8%)
  local copies, waits for them, and re-layouts  2.81 us (2%)
    all_to_all x3, waiting for transfers between devices, exchange(): return lax.all_to_all(array, 'ctx', split_axis=0, concat_axis=0, tiled=True)  54 us
    all_to_all x1, blocking collectives, exchange(): return lax.all_to_all(array, 'ctx', split_axis=0, concat_axis=0, tiled=True)  20.6 us
    all_to_all x3, starting transfers between devices, exchange(): return lax.all_to_all(array, 'ctx', split_axis=0, concat_axis=0, tiled=True)  18.6 us
    pallas_call x4, Pallas kernels, call(): pl.pallas_call(kernel, in_specs=[there] * len(stored) + [pl.BlockSpec(mem...  16.8 us
    ppermute x3, waiting for transfers between devices, send(): lax.ppermute(piece, 'fsdp', [(m, (m + shift) % members) for m in range(me...  6.81 us
    convert_element_type x2, other arithmetic, local_table(): return jnp.where(keep[None], cosine(step, length), 0.0).astype(jnp.bfloat16)  5.73 us
    ppermute x3, starting transfers between devices, send(): lax.ppermute(piece, 'fsdp', [(m, (m + shift) % members) for m in range(me...  4.91 us
    convert_element_type x2, other arithmetic, cross_table(): jnp.where(same, cosine(step, 2 * devices) * SPREAD, 0.0)  4.83 us
  transfers between devices with their start and end apart: 6, of which 4 were waited for; matrix products, arithmetic and copies ran while one was open for 8% of the time, Pallas kernels for 2%

profile of v1, /device:TPU:1, one launch (start us, length us, event | category | flops | bytes accessed | tf_op | source)
XLA Modules:
  0.0 137.4 jit_solution(8904523231676485681)
XLA Ops:
  0.0 2.8 %shard_map.55 = (bf16[512,1024]{1,0:T(8,128)(2,1)}, bf16[2,256,1024]{2,1,0:T(8,128)(2,1)}) custom-call(bf16[512,1024]{1,0:T(8,128)(2,1)} %left_hbm.1, bf16[512,1024]{1,0:T(8,128)(2,1)} %right_hbm.1, bf16[2,256,4096]{2,1,0:T(8,128)(2,1)} %own_hbm.1), custom_call_target="tpu_custom_call" | custom-call | tf_op jit(solution)/shard_map/pallas_call | solution.py:231
  2.8 2.8 %constant_dynamic-slice_fusion = (bf16[2,256,1024]{2,1,0:T(8,128)(2,1)S(1)}, bf16[2,256,1024]{2,1,0:T(8,128)(2,1)}) fusion(bf16[2,256,4096]{2,1,0:T(8,128)(2,1)} %own_hbm.1, s32[]{:T(128)S(6)} %select_n.443, s32[]{:T(128)S(6)} %select_n.442), kind=kLoop, calls=%fused_computation.126 | loop fusion | bytes 4194312 | tf_op jit(solution)/shard_map/dynamic_slice | solution.py:345
  5.6 2.0 %collective-permute-start = (bf16[2,256,1024]{2,1,0:T(8,128)(2,1)}, bf16[2,256,1024]{2,1,0:T(8,128)(2,1)}, u32[]{:S(2)}, u32[]{:S(2)}) collective-permute-start(bf16[2,256,1024]{2,1,0:T(8,128)(2,1)} %get-tuple-element.16), channel_id=1, source_target_pairs={{0,1},{1,2},{2,3},{3,0},{4,5},{5,6},{6,7},{7,4},{8,9},{9,10},{10,1... | collective-permute-start | bytes 3145736 | tf_op jit(solution)/shard_map/ppermute | solution.py:348
  7.7 1.3 collective-permute-start.2
  8.9 9.5 %all-to-all-start = ((bf16[32,16,1024]{2,1,0:T(8,128)(2,1)}), bf16[32,16,1024]{2,1,0:T(8,128)(2,1)S(1)}, u32[]{:S(2)}, u32[]{:S(2)}) async-start(bf16[32,16,1024]{2,1,0:T(8,128)(2,1)} %bitcast), calls=%async_computation | async-start | bytes 2097152 | tf_op jit(solution)/shard_map/all_to_all | solution.py:331
  18.5 1.6 %collective-permute-start.1 = (bf16[2,256,1024]{2,1,0:T(8,128)(2,1)}, bf16[2,256,1024]{2,1,0:T(8,128)(2,1)}, u32[]{:S(2)}, u32[]{:S(2)}) collective-permute-start(bf16[2,256,1024]{2,1,0:T(8,128)(2,1)} %get-tuple-element.13), channel_id=1, source_target_pairs={{0,2},{1,3},{2,0},{3,1},{4,6},{5,7},{6,4},{7,5},{8,10},{9,11},{10,... | collective-permute-start | bytes 3145736 | tf_op jit(solution)/shard_map/ppermute | solution.py:348
  20.2 0.2 compare_or_fusion
  20.3 2.3 %select_convert_fusion.table_ref = bf16[1024,512]{1,0:T(8,128)(2,1)S(1)} fusion(s32[1024]{0:T(1024)S(1)} %get-tuple-element.17, s32[512]{0:T(512)S(1)} %get-tuple-element.19, s32[1024]{0:T(1024)S(1)} %get-tuple-element.18, s32[512]{0:T(512)S(1)} %get-tuple-element.20, s32[1024]{0:T(1024)S(1)} %fusion.23), kind=kLoop, calls=%fused_computation | loop fusion | flops 14155776 | bytes 1064960 | tf_op jit(solution)/shard_map/convert_element_type | solution.py:48
  22.7 12.7 %all-to-all-done = bf16[32,16,1024]{2,1,0:T(8,128)(2,1)S(1)} async-done(((bf16[32,16,1024]{2,1,0:T(8,128)(2,1)}), bf16[32,16,1024]{2,1,0:T(8,128)(2,1)S(1)}, u32[]{:S(2)}, u32[]{:S(2)}) %all-to-all-start) | async-done | bytes 1048608 | tf_op jit(solution)/shard_map/all_to_all | solution.py:331
  35.4 2.5 %shard_map.56 = bf16[1024,1024]{1,0:T(8,128)(2,1)} custom-call(bf16[1024,512]{1,0:T(8,128)(2,1)S(1)} %select_convert_fusion.table_ref, bf16[512,1024]{1,0:T(8,128)(2,1)S(1)} %bitcast.11), custom_call_target="tpu_custom_call" | custom-call | tf_op jit(solution)/shard_map/pallas_call | solution.py:231
  37.8 4.6 %all-to-all-start.1 = ((bf16[32,32,1024]{2,1,0:T(8,128)(2,1)}), bf16[32,32,1024]{2,1,0:T(8,128)(2,1)}, u32[]{:S(2)}, u32[]{:S(2)}) async-start(bf16[32,32,1024]{2,1,0:T(8,128)(2,1)} %bitcast.2), calls=%async_computation.1 | async-start | bytes 4194304 | tf_op jit(solution)/shard_map/all_to_all | solution.py:331
  42.4 0.2 compare_or_fusion.1
  42.7 0.1 subtract_multiply_fusion
  42.8 0.1 subtract_multiply_fusion.1
  42.9 2.9 %select_convert_fusion.2.m_hbm = bf16[4,512,256]{2,1,0:T(8,128)(2,1)} fusion(s32[512,256]{1,0:T(8,128)S(1)} %subtract_multiply_fusion.1, s32[512]{0:T(512)S(1)} %fusion.37, s32[4,256]{1,0:T(4,128)S(1)} %iota_add_fusion, pred[512,256]{1,0:T(8,128)(4,1)S(1)} %compare_or_fusion.1), kind=kLoop, calls=%fused_computation.18 | loop fusion | flops 13107200 | bytes 1710080 | tf_op jit(solution)/shard_map/convert_element_type | solution.py:75
  45.9 2.8 %select_convert_fusion.1.g_hbm = bf16[4,256,512]{2,1,0:T(8,128)(2,1)} fusion(s32[256,512]{1,0:T(8,128)S(1)} %subtract_multiply_fusion, s32[512]{0:T(512)S(1)} %fusion.37, s32[4,256]{1,0:T(4,128)S(1)} %iota_add_fusion, pred[256,512]{1,0:T(8,128)(4,1)S(1)} %compare_or_fusion), kind=kLoop, calls=%fused_computation.9 | loop fusion | flops 13107200 | bytes 1710080 | tf_op jit(solution)/shard_map/convert_element_type | solution.py:75
  48.7 0.0 collective-permute-done.near_hbm
  48.7 0.0 collective-permute-done.2.last_hbm
  48.7 6.8 %collective-permute-done.1.far_hbm = bf16[2,256,1024]{2,1,0:T(8,128)(2,1)} collective-permute-done((bf16[2,256,1024]{2,1,0:T(8,128)(2,1)}, bf16[2,256,1024]{2,1,0:T(8,128)(2,1)}, u32[]{:S(2)}, u32[]{:S(2)}) %collective-permute-start.1) | collective-permute-done | bytes 1048608 | tf_op jit(solution)/shard_map/ppermute | solution.py:348
  55.5 15.3 %all-to-all-done.1 = bf16[32,32,1024]{2,1,0:T(8,128)(2,1)} async-done(((bf16[32,32,1024]{2,1,0:T(8,128)(2,1)}), bf16[32,32,1024]{2,1,0:T(8,128)(2,1)}, u32[]{:S(2)}, u32[]{:S(2)}) %all-to-all-start.1) | async-done | bytes 2097184 | tf_op jit(solution)/shard_map/all_to_all | solution.py:331
  70.8 9.1 %shard_map.57 = bf16[32,4,8,1024]{3,2,1,0:T(8,128)(2,1)} custom-call(bf16[4,512,256]{2,1,0:T(8,128)(2,1)} %select_convert_fusion.2.m_hbm, bf16[4,256,512]{2,1,0:T(8,128)(2,1)} %select_convert_fusion.1.g_hbm, bf16[2,256,4096]{2,1,0:T(8,128)(2,1)} %own_hbm.1, bf16[2,256,1024]{2,1,0:T(8,128)(2,1)} %collective-permute-done.near_hbm, ...), custom_call_target="tpu_custom_call" | custom-call | tf_op jit(solution)/shard_map/pallas_call | solution.py:231
  79.9 4.5 %all-to-all-start.2 = ((bf16[32,32,1024]{2,1,0:T(8,128)(2,1)}), bf16[32,32,1024]{2,1,0:T(8,128)(2,1)S(1)}, u32[]{:S(2)}, u32[]{:S(2)}) async-start(bf16[32,32,1024]{2,1,0:T(8,128)(2,1)} %bitcast.14), calls=%async_computation.2 | async-start | bytes 4194304 | tf_op jit(solution)/shard_map/all_to_all | solution.py:331
  84.4 2.5 %select_convert_fusion.3.table_ref = bf16[512,1024]{1,0:T(8,128)(2,1)S(1)} fusion(s32[1024]{0:T(1024)S(1)} %get-tuple-element.17, s32[1024]{0:T(1024)S(1)} %get-tuple-element.18, s32[512]{0:T(512)S(1)} %get-tuple-element.19, s32[1024]{0:T(1024)S(1)} %fusion.23, s32[512]{0:T(512)S(1)} %get-tuple-element.20), kind=kLoop, calls=%fused_computation.27 | loop fusion | flops 14155776 | bytes 1064960 | tf_op jit(solution)/shard_map/convert_element_type | solution.py:48
  86.9 25.9 %all-to-all-done.2 = bf16[32,32,1024]{2,1,0:T(8,128)(2,1)S(1)} async-done(((bf16[32,32,1024]{2,1,0:T(8,128)(2,1)}), bf16[32,32,1024]{2,1,0:T(8,128)(2,1)S(1)}, u32[]{:S(2)}, u32[]{:S(2)}) %all-to-all-start.2) | async-done | bytes 2097184 | tf_op jit(solution)/shard_map/all_to_all | solution.py:331
  112.9 1.4 %fold.1 = bf16[512,1024]{1,0:T(8,128)(2,1)S(1)} custom-call(bf16[512,1024]{1,0:T(8,128)(2,1)S(1)} %select_convert_fusion.3.table_ref, bf16[1024,1024]{1,0:T(8,128)(2,1)S(1)} %bitcast.9), custom_call_target="tpu_custom_call" | custom-call | tf_op jit(solution)/shard_map/fold/pallas_call | solution.py:249
  114.3 0.0 copy-start
  114.3 0.0 copy-start.1
  114.3 20.6 %all_to_all.20 = bf16[32,16,1024]{2,1,0:T(8,128)(2,1)S(1)} all-to-all(bf16[32,16,1024]{2,1,0:T(8,128)(2,1)S(1)} %bitcast.12), channel_id=1, replica_groups=mesh['ctx'=32,'fsdp'=4] {'ctx'}, dimensions={0} | all-to-all | bytes 2097152 | tf_op jit(solution)/shard_map/all_to_all | solution.py:331
  135.0 0.0 copy-done
  135.0 0.0 copy-done.1
  135.0 2.4 %shard_map.58 = bf16[512,1024]{1,0:T(8,128)(2,1)} custom-call(bf16[512,1024]{1,0:T(8,128)(2,1)S(1)} %bitcast.10, bf16[512,1024]{1,0:T(8,128)(2,1)} %get-tuple-element.14.mixed_ref, bf16[512,1024]{1,0:T(8,128)(2,1)S(1)} %copy-done, f32[1,1024]{1,0:T(1,128)S(1)} %bitcast.13), custom_call_target="tpu_custom_call" | custom-call | tf_op jit(solution)/shard_map/pallas_call | solution.py:231
  (11 shorter events, 0.1 us)
Async XLA Ops:
  5.6 43.0 %collective-permute-start = (bf16[2,256,1024]{2,1,0:T(8,128)(2,1)}, bf16[2,256,1024]{2,1,0:T(8,128)(2,1)}, u32[]{:S(2)}, u32[]{:S(2)}) collective-permute-start(bf16[2,256,1024]{2,1,0:T(8,128)(2,1)} %get-tuple-element.16), channel_id=1, source_target_pairs={{0,1},{1,2},{2,3},{3,0},{4,5},{5,6},{6,7},{7,4},{8,9},{9,10},{10,1... | collective-permute-start | bytes 3145736 | tf_op jit(solution)/shard_map/ppermute | solution.py:348
  7.7 41.0 %collective-permute-start.2 = (bf16[2,256,1024]{2,1,0:T(8,128)(2,1)S(1)}, bf16[2,256,1024]{2,1,0:T(8,128)(2,1)}, u32[]{:S(2)}, u32[]{:S(2)}) collective-permute-start(bf16[2,256,1024]{2,1,0:T(8,128)(2,1)S(1)} %get-tuple-element.15), channel_id=1, source_target_pairs={{0,3},{1,0},{2,1},{3,2},{4,7},{5,4},{6,5},{7,6},{8,11},{9,8},{10,9... | collective-permute-start | bytes 3145736 | tf_op jit(solution)/shard_map/ppermute | solution.py:348
  8.9 26.4 %all-to-all-start = ((bf16[32,16,1024]{2,1,0:T(8,128)(2,1)}), bf16[32,16,1024]{2,1,0:T(8,128)(2,1)S(1)}, u32[]{:S(2)}, u32[]{:S(2)}) async-start(bf16[32,16,1024]{2,1,0:T(8,128)(2,1)} %bitcast), calls=%async_computation | async-start | bytes 2097152 | tf_op jit(solution)/shard_map/all_to_all | solution.py:331
  18.5 37.0 %collective-permute-start.1 = (bf16[2,256,1024]{2,1,0:T(8,128)(2,1)}, bf16[2,256,1024]{2,1,0:T(8,128)(2,1)}, u32[]{:S(2)}, u32[]{:S(2)}) collective-permute-start(bf16[2,256,1024]{2,1,0:T(8,128)(2,1)} %get-tuple-element.13), channel_id=1, source_target_pairs={{0,2},{1,3},{2,0},{3,1},{4,6},{5,7},{6,4},{7,5},{8,10},{9,11},{10,... | collective-permute-start | bytes 3145736 | tf_op jit(solution)/shard_map/ppermute | solution.py:348
  37.8 32.9 %all-to-all-start.1 = ((bf16[32,32,1024]{2,1,0:T(8,128)(2,1)}), bf16[32,32,1024]{2,1,0:T(8,128)(2,1)}, u32[]{:S(2)}, u32[]{:S(2)}) async-start(bf16[32,32,1024]{2,1,0:T(8,128)(2,1)} %bitcast.2), calls=%async_computation.1 | async-start | bytes 4194304 | tf_op jit(solution)/shard_map/all_to_all | solution.py:331
  79.9 32.9 %all-to-all-start.2 = ((bf16[32,32,1024]{2,1,0:T(8,128)(2,1)}), bf16[32,32,1024]{2,1,0:T(8,128)(2,1)S(1)}, u32[]{:S(2)}, u32[]{:S(2)}) async-start(bf16[32,32,1024]{2,1,0:T(8,128)(2,1)} %bitcast.14), calls=%async_computation.2 | async-start | bytes 4194304 | tf_op jit(solution)/shard_map/all_to_all | solution.py:331
  114.3 20.7 %copy-start = (bf16[512,1024]{1,0:T(8,128)(2,1)S(1)}, bf16[512,1024]{1,0:T(8,128)(2,1)}, u32[]{:S(2)}) copy-start(bf16[512,1024]{1,0:T(8,128)(2,1)} %gate_ref.1) | copy-start | bytes 3145732
  114.3 20.7 %copy-start.1 = (f32[1024]{0:T(1024)S(1)}, f32[1024]{0:T(1024)}, u32[]{:S(2)}) copy-start(f32[1024]{0:T(1024)} %param.8) | copy-start | bytes 12292

commit v2 on v1

--- a/solution.py
+++ b/solution.py
@@ -106,7 +106,7 @@
 
 def local_kernel(
     m_hbm, g_hbm, own_hbm, near_hbm, far_hbm, last_hbm, x_hbm, o_hbm,
-    m_ref, g_ref, r_ref, x_ref, o_ref, b_ref, m_sem, g_sem, r_sem, x_sem, o_sem,
+    m_ref, g_ref, r_ref, x_ref, o_ref, b_ref, mirrors, m_sem, g_sem, r_sem, x_sem, o_sem,
 ):
     quart, width = r_ref.shape[2] // 2, r_ref.shape[3]
     first = lax.axis_index("ctx") == 0
@@ -129,11 +129,7 @@
         there = jnp.where(first, 2 * group + 1, members - 1 - group)
         here = lax.rem(member + members - here, members)
         there = lax.rem(member + members - there, members)
-        size = 2 * quart
-        row = lax.broadcasted_iota(jnp.int32, (size, size), 0)
-        col = lax.broadcasted_iota(jnp.int32, (size, size), 1)
-        shifted = jnp.where(first, 1, 0) if group == 0 else 0
-        mirror = jnp.where(row + col == size - 1 + shifted, 0.5, 0.0).astype(jnp.bfloat16)
+        mirror = mirrors[group]
         even = 0.5 * r_ref[here, 0, :, cols].astype(jnp.float32) + jnp.dot(
             mirror, r_ref[there, 0, :, cols], preferred_element_type=jnp.float32
         )
@@ -145,8 +141,8 @@
     def incoming(i, cols):
         return pltpu.make_async_copy(x_hbm.at[:, :, :, cols], x_ref.at[:, :, :, cols], x_sem.at[i])
 
-    def store(i, cols):
-        return pltpu.make_async_copy(o_ref.at[:, :, :, cols], o_hbm.at[:, :, :, cols], o_sem.at[i])
+    def store(digit, i, cols):
+        return pltpu.make_async_copy(o_ref.at[:, digit, :, cols], o_hbm.at[:, digit, :, cols], o_sem.at[digit, i])
 
     def start(copies):
         for copy in copies:
@@ -161,6 +157,14 @@
         incoming(i, pl.ds(i * LANES, LANES)).start()
         start(filters(i, pl.ds(i * LANES, LANES)))
     backward.start()
+
+    size = 2 * quart
+    row = lax.broadcasted_iota(jnp.int32, (size, size), 0)
+    col = lax.broadcasted_iota(jnp.int32, (size, size), 1)
+    for group in range(2):
+        shifted = jnp.where(first, 1, 0) if group == 0 else 0
+        mirrors[group] = jnp.where(row + col == size - 1 + shifted, 0.5, 0.0).astype(mirrors.dtype)
+
     forward.wait()
 
     def ahead(i, cols):
@@ -201,12 +205,13 @@
         for digit in range(RADIX):
             y = jnp.dot(g_ref[digit], b_ref[digit, :, cols], preferred_element_type=jnp.float32)
             o_ref[:, digit, :, cols] = y.reshape(o_ref.shape[0], o_ref.shape[2], -1).astype(o_ref.dtype)
-        store(i, cols).start()
+            store(digit, i, cols).start()
 
     each_block(width, ahead)
     backward.wait()
     each_block(width, back)
-    each_block(width, lambda i, cols: store(i, cols).wait())
+    for digit in range(RADIX):
+        each_block(width, lambda i, cols, digit=digit: store(digit, i, cols).wait())
 
 
 def gate_kernel(restored_ref, mixed_ref, gate_ref, bias_ref, o_hbm, o_buf, o_sem):
@@ -263,8 +268,8 @@
     stored = pltpu.VMEM((len(pieces), *pieces[1].shape), x.dtype)
     scratch = [pltpu.VMEM(forward.shape, x.dtype), pltpu.VMEM(backward.shape, x.dtype), stored]
     scratch += [pltpu.VMEM(x.shape, x.dtype), pltpu.VMEM(x.shape, x.dtype)]
-    scratch += [pltpu.VMEM((RADIX, rows, x.shape[-1]), x.dtype)]
-    scratch += [dma(()), dma(()), dma((len(pieces), count)), dma((count,)), dma((count,))]
+    scratch += [pltpu.VMEM((RADIX, rows, x.shape[-1]), x.dtype), pltpu.VMEM((2, rows // 2, rows // 2), x.dtype)]
+    scratch += [dma(()), dma(()), dma((len(pieces), count)), dma((count,)), dma((RADIX, count))]
     out = jax.ShapeDtypeStruct(x.shape, x.dtype)
     return call(local_kernel, (forward, backward, *pieces, x), (), out, scratch, 62)
 
@@ -288,9 +293,6 @@
         at = pl.ds(i * rows, rows)
         return pltpu.make_async_copy(o_buf.at[at], o_hbm.at[at], o_sem.at[i])
 
-    for i in range(blocks):
-        for load in loads(i):
-            load.start()
     mine = pl.ds(pl.multiple_of(target * width, width), width)
     parts = range(far_buf.shape[0])
     taken = [pltpu.make_async_copy(stored_hbm.at[p, :, mine], far_buf.at[p], far_sem.at[0, p]) for p in parts]
@@ -299,13 +301,16 @@
         copy.start()
     for i in range(blocks):
         for load in loads(i):
+            load.start()
+    for p in parts:
+        taken[p].wait()
+        given[p].start()
+    for i in range(blocks):
+        for load in loads(i):
             load.wait()
         at = slice(i * rows, (i + 1) * rows)
         o_buf[at] = (left[at].astype(jnp.float32) * right[at].astype(jnp.float32)).astype(o_buf.dtype)
         store(i).start()
-    for p in parts:
-        taken[p].wait()
-        given[p].start()
     for i in range(blocks):
         store(i).wait()
     for copy in given:

time: 138 us -> 138 us (level)
  no operation moved by 1% of the time
where the time goes in v2:
time: 138 us
  waiting for transfers between devices  60.8 us (44%)
  starting transfers between devices  23.5 us (17%)
  blocking collectives  20.6 us (15%)
  Pallas kernels  18.3 us (13%)
  other arithmetic  11.2 us (8%)
  local copies, waits for them, and re-layouts  2.81 us (2%)
    all_to_all x3, waiting for transfers between devices, exchange(): return lax.all_to_all(array, 'ctx', split_axis=0, concat_axis=0, tiled=True)  54 us
    all_to_all x1, blocking collectives, exchange(): return lax.all_to_all(array, 'ctx', split_axis=0, concat_axis=0, tiled=True)  20.6 us
    all_to_all x3, starting transfers between devices, exchange(): return lax.all_to_all(array, 'ctx', split_axis=0, concat_axis=0, tiled=True)  18.6 us
    pallas_call x4, Pallas kernels, call(): pl.pallas_call(kernel, in_specs=[there] * len(stored) + [pl.BlockSpec(mem...  16.9 us
    ppermute x3, waiting for transfers between devices, send(): lax.ppermute(piece, 'fsdp', [(m, (m + shift) % members) for m in range(me...  6.81 us
    convert_element_type x2, other arithmetic, local_table(): return jnp.where(keep[None], cosine(step, length), 0.0).astype(jnp.bfloat16)  5.73 us
    ppermute x3, starting transfers between devices, send(): lax.ppermute(piece, 'fsdp', [(m, (m + shift) % members) for m in range(me...  4.91 us
    convert_element_type x2, other arithmetic, cross_table(): jnp.where(same, cosine(step, 2 * devices) * SPREAD, 0.0)  4.83 us
  transfers between devices with their start and end apart: 6, of which 4 were waited for; matrix products, arithmetic and copies ran while one was open for 8% of the time, Pallas kernels for 2%

profile of v2, /device:TPU:1, one launch (start us, length us, event | category | flops | bytes accessed | tf_op | source)
XLA Modules:
  0.0 137.7 jit_solution(9468616269379529802)
XLA Ops:
  0.0 3.1 %shard_map.55 = (bf16[512,1024]{1,0:T(8,128)(2,1)}, bf16[2,256,1024]{2,1,0:T(8,128)(2,1)}) custom-call(bf16[512,1024]{1,0:T(8,128)(2,1)} %left_hbm.1, bf16[512,1024]{1,0:T(8,128)(2,1)} %right_hbm.1, bf16[2,256,4096]{2,1,0:T(8,128)(2,1)} %own_hbm.1), custom_call_target="tpu_custom_call" | custom-call | tf_op jit(solution)/shard_map/pallas_call | solution.py:236
  3.2 2.8 %constant_dynamic-slice_fusion = (bf16[2,256,1024]{2,1,0:T(8,128)(2,1)S(1)}, bf16[2,256,1024]{2,1,0:T(8,128)(2,1)}) fusion(bf16[2,256,4096]{2,1,0:T(8,128)(2,1)} %own_hbm.1, s32[]{:T(128)S(6)} %select_n.443, s32[]{:T(128)S(6)} %select_n.442), kind=kLoop, calls=%fused_computation.126 | loop fusion | bytes 4194312 | tf_op jit(solution)/shard_map/dynamic_slice | solution.py:350
  6.0 2.0 %collective-permute-start = (bf16[2,256,1024]{2,1,0:T(8,128)(2,1)}, bf16[2,256,1024]{2,1,0:T(8,128)(2,1)}, u32[]{:S(2)}, u32[]{:S(2)}) collective-permute-start(bf16[2,256,1024]{2,1,0:T(8,128)(2,1)} %get-tuple-element.16), channel_id=1, source_target_pairs={{0,1},{1,2},{2,3},{3,0},{4,5},{5,6},{6,7},{7,4},{8,9},{9,10},{10,1... | collective-permute-start | bytes 3145736 | tf_op jit(solution)/shard_map/ppermute | solution.py:353
  8.0 1.3 collective-permute-start.2
  9.3 9.5 %all-to-all-start = ((bf16[32,16,1024]{2,1,0:T(8,128)(2,1)}), bf16[32,16,1024]{2,1,0:T(8,128)(2,1)S(1)}, u32[]{:S(2)}, u32[]{:S(2)}) async-start(bf16[32,16,1024]{2,1,0:T(8,128)(2,1)} %bitcast), calls=%async_computation | async-start | bytes 2097152 | tf_op jit(solution)/shard_map/all_to_all | solution.py:336
  18.8 1.6 %collective-permute-start.1 = (bf16[2,256,1024]{2,1,0:T(8,128)(2,1)}, bf16[2,256,1024]{2,1,0:T(8,128)(2,1)}, u32[]{:S(2)}, u32[]{:S(2)}) collective-permute-start(bf16[2,256,1024]{2,1,0:T(8,128)(2,1)} %get-tuple-element.13), channel_id=1, source_target_pairs={{0,2},{1,3},{2,0},{3,1},{4,6},{5,7},{6,4},{7,5},{8,10},{9,11},{10,... | collective-permute-start | bytes 3145736 | tf_op jit(solution)/shard_map/ppermute | solution.py:353
  20.5 0.2 compare_or_fusion
  20.6 2.3 %select_convert_fusion.table_ref = bf16[1024,512]{1,0:T(8,128)(2,1)S(1)} fusion(s32[1024]{0:T(1024)S(1)} %get-tuple-element.17, s32[512]{0:T(512)S(1)} %get-tuple-element.19, s32[1024]{0:T(1024)S(1)} %get-tuple-element.18, s32[512]{0:T(512)S(1)} %get-tuple-element.20, s32[1024]{0:T(1024)S(1)} %fusion.23), kind=kLoop, calls=%fused_computation | loop fusion | flops 14155776 | bytes 1064960 | tf_op jit(solution)/shard_map/convert_element_type | solution.py:48
  23.0 12.7 %all-to-all-done = bf16[32,16,1024]{2,1,0:T(8,128)(2,1)S(1)} async-done(((bf16[32,16,1024]{2,1,0:T(8,128)(2,1)}), bf16[32,16,1024]{2,1,0:T(8,128)(2,1)S(1)}, u32[]{:S(2)}, u32[]{:S(2)}) %all-to-all-start) | async-done | bytes 1048608 | tf_op jit(solution)/shard_map/all_to_all | solution.py:336
  35.7 2.5 %shard_map.56 = bf16[1024,1024]{1,0:T(8,128)(2,1)} custom-call(bf16[1024,512]{1,0:T(8,128)(2,1)S(1)} %select_convert_fusion.table_ref, bf16[512,1024]{1,0:T(8,128)(2,1)S(1)} %bitcast.11), custom_call_target="tpu_custom_call" | custom-call | tf_op jit(solution)/shard_map/pallas_call | solution.py:236
  38.2 4.6 %all-to-all-start.1 = ((bf16[32,32,1024]{2,1,0:T(8,128)(2,1)}), bf16[32,32,1024]{2,1,0:T(8,128)(2,1)}, u32[]{:S(2)}, u32[]{:S(2)}) async-start(bf16[32,32,1024]{2,1,0:T(8,128)(2,1)} %bitcast.2), calls=%async_computation.1 | async-start | bytes 4194304 | tf_op jit(solution)/shard_map/all_to_all | solution.py:336
  42.8 0.2 compare_or_fusion.1
  43.0 0.1 subtract_multiply_fusion
  43.1 0.1 subtract_multiply_fusion.1
  43.3 2.9 %select_convert_fusion.2.m_hbm = bf16[4,512,256]{2,1,0:T(8,128)(2,1)} fusion(s32[512,256]{1,0:T(8,128)S(1)} %subtract_multiply_fusion.1, s32[512]{0:T(512)S(1)} %fusion.37, s32[4,256]{1,0:T(4,128)S(1)} %iota_add_fusion, pred[512,256]{1,0:T(8,128)(4,1)S(1)} %compare_or_fusion.1), kind=kLoop, calls=%fused_computation.18 | loop fusion | flops 13107200 | bytes 1710080 | tf_op jit(solution)/shard_map/convert_element_type | solution.py:75
  46.2 2.8 %select_convert_fusion.1.g_hbm = bf16[4,256,512]{2,1,0:T(8,128)(2,1)} fusion(s32[256,512]{1,0:T(8,128)S(1)} %subtract_multiply_fusion, s32[512]{0:T(512)S(1)} %fusion.37, s32[4,256]{1,0:T(4,128)S(1)} %iota_add_fusion, pred[256,512]{1,0:T(8,128)(4,1)S(1)} %compare_or_fusion), kind=kLoop, calls=%fused_computation.9 | loop fusion | flops 13107200 | bytes 1710080 | tf_op jit(solution)/shard_map/convert_element_type | solution.py:75
  49.0 0.0 collective-permute-done.near_hbm
  49.0 0.0 collective-permute-done.2.last_hbm
  49.0 6.8 %collective-permute-done.1.far_hbm = bf16[2,256,1024]{2,1,0:T(8,128)(2,1)} collective-permute-done((bf16[2,256,1024]{2,1,0:T(8,128)(2,1)}, bf16[2,256,1024]{2,1,0:T(8,128)(2,1)}, u32[]{:S(2)}, u32[]{:S(2)}) %collective-permute-start.1) | collective-permute-done | bytes 1048608 | tf_op jit(solution)/shard_map/ppermute | solution.py:353
  55.8 15.3 %all-to-all-done.1 = bf16[32,32,1024]{2,1,0:T(8,128)(2,1)} async-done(((bf16[32,32,1024]{2,1,0:T(8,128)(2,1)}), bf16[32,32,1024]{2,1,0:T(8,128)(2,1)}, u32[]{:S(2)}, u32[]{:S(2)}) %all-to-all-start.1) | async-done | bytes 2097184 | tf_op jit(solution)/shard_map/all_to_all | solution.py:336
  71.1 8.9 %shard_map.57 = bf16[32,4,8,1024]{3,2,1,0:T(8,128)(2,1)} custom-call(bf16[4,512,256]{2,1,0:T(8,128)(2,1)} %select_convert_fusion.2.m_hbm, bf16[4,256,512]{2,1,0:T(8,128)(2,1)} %select_convert_fusion.1.g_hbm, bf16[2,256,4096]{2,1,0:T(8,128)(2,1)} %own_hbm.1, bf16[2,256,1024]{2,1,0:T(8,128)(2,1)} %collective-permute-done.near_hbm, ...), custom_call_target="tpu_custom_call" | custom-call | tf_op jit(solution)/shard_map/pallas_call | solution.py:236
  80.0 4.5 %all-to-all-start.2 = ((bf16[32,32,1024]{2,1,0:T(8,128)(2,1)}), bf16[32,32,1024]{2,1,0:T(8,128)(2,1)S(1)}, u32[]{:S(2)}, u32[]{:S(2)}) async-start(bf16[32,32,1024]{2,1,0:T(8,128)(2,1)} %bitcast.14), calls=%async_computation.2 | async-start | bytes 4194304 | tf_op jit(solution)/shard_map/all_to_all | solution.py:336
  84.5 2.5 %select_convert_fusion.3.table_ref = bf16[512,1024]{1,0:T(8,128)(2,1)S(1)} fusion(s32[1024]{0:T(1024)S(1)} %get-tuple-element.17, s32[1024]{0:T(1024)S(1)} %get-tuple-element.18, s32[512]{0:T(512)S(1)} %get-tuple-element.19, s32[1024]{0:T(1024)S(1)} %fusion.23, s32[512]{0:T(512)S(1)} %get-tuple-element.20), kind=kLoop, calls=%fused_computation.27 | loop fusion | flops 14155776 | bytes 1064960 | tf_op jit(solution)/shard_map/convert_element_type | solution.py:48
  87.0 25.9 %all-to-all-done.2 = bf16[32,32,1024]{2,1,0:T(8,128)(2,1)S(1)} async-done(((bf16[32,32,1024]{2,1,0:T(8,128)(2,1)}), bf16[32,32,1024]{2,1,0:T(8,128)(2,1)S(1)}, u32[]{:S(2)}, u32[]{:S(2)}) %all-to-all-start.2) | async-done | bytes 2097184 | tf_op jit(solution)/shard_map/all_to_all | solution.py:336
  113.0 1.4 %fold.1 = bf16[512,1024]{1,0:T(8,128)(2,1)S(1)} custom-call(bf16[512,1024]{1,0:T(8,128)(2,1)S(1)} %select_convert_fusion.3.table_ref, bf16[1024,1024]{1,0:T(8,128)(2,1)S(1)} %bitcast.9), custom_call_target="tpu_custom_call" | custom-call | tf_op jit(solution)/shard_map/fold/pallas_call | solution.py:254
  114.4 0.0 copy-start
  114.4 0.0 copy-start.1
  114.4 20.6 %all_to_all.20 = bf16[32,16,1024]{2,1,0:T(8,128)(2,1)S(1)} all-to-all(bf16[32,16,1024]{2,1,0:T(8,128)(2,1)S(1)} %bitcast.12), channel_id=1, replica_groups=mesh['ctx'=32,'fsdp'=4] {'ctx'}, dimensions={0} | all-to-all | bytes 2097152 | tf_op jit(solution)/shard_map/all_to_all | solution.py:336
  135.1 0.0 copy-done
  135.1 0.0 copy-done.1
  135.1 2.4 %shard_map.58 = bf16[512,1024]{1,0:T(8,128)(2,1)} custom-call(bf16[512,1024]{1,0:T(8,128)(2,1)S(1)} %bitcast.10, bf16[512,1024]{1,0:T(8,128)(2,1)} %get-tuple-element.14.mixed_ref, bf16[512,1024]{1,0:T(8,128)(2,1)S(1)} %copy-done, f32[1,1024]{1,0:T(1,128)S(1)} %bitcast.13), custom_call_target="tpu_custom_call" | custom-call | tf_op jit(solution)/shard_map/pallas_call | solution.py:236
  (11 shorter events, 0.1 us)
Async XLA Ops:
  6.0 43.0 %collective-permute-start = (bf16[2,256,1024]{2,1,0:T(8,128)(2,1)}, bf16[2,256,1024]{2,1,0:T(8,128)(2,1)}, u32[]{:S(2)}, u32[]{:S(2)}) collective-permute-start(bf16[2,256,1024]{2,1,0:T(8,128)(2,1)} %get-tuple-element.16), channel_id=1, source_target_pairs={{0,1},{1,2},{2,3},{3,0},{4,5},{5,6},{6,7},{7,4},{8,9},{9,10},{10,1... | collective-permute-start | bytes 3145736 | tf_op jit(solution)/shard_map/ppermute | solution.py:353
  8.0 41.0 %collective-permute-start.2 = (bf16[2,256,1024]{2,1,0:T(8,128)(2,1)S(1)}, bf16[2,256,1024]{2,1,0:T(8,128)(2,1)}, u32[]{:S(2)}, u32[]{:S(2)}) collective-permute-start(bf16[2,256,1024]{2,1,0:T(8,128)(2,1)S(1)} %get-tuple-element.15), channel_id=1, source_target_pairs={{0,3},{1,0},{2,1},{3,2},{4,7},{5,4},{6,5},{7,6},{8,11},{9,8},{10,9... | collective-permute-start | bytes 3145736 | tf_op jit(solution)/shard_map/ppermute | solution.py:353
  9.3 26.4 %all-to-all-start = ((bf16[32,16,1024]{2,1,0:T(8,128)(2,1)}), bf16[32,16,1024]{2,1,0:T(8,128)(2,1)S(1)}, u32[]{:S(2)}, u32[]{:S(2)}) async-start(bf16[32,16,1024]{2,1,0:T(8,128)(2,1)} %bitcast), calls=%async_computation | async-start | bytes 2097152 | tf_op jit(solution)/shard_map/all_to_all | solution.py:336
  18.8 37.0 %collective-permute-start.1 = (bf16[2,256,1024]{2,1,0:T(8,128)(2,1)}, bf16[2,256,1024]{2,1,0:T(8,128)(2,1)}, u32[]{:S(2)}, u32[]{:S(2)}) collective-permute-start(bf16[2,256,1024]{2,1,0:T(8,128)(2,1)} %get-tuple-element.13), channel_id=1, source_target_pairs={{0,2},{1,3},{2,0},{3,1},{4,6},{5,7},{6,4},{7,5},{8,10},{9,11},{10,... | collective-permute-start | bytes 3145736 | tf_op jit(solution)/shard_map/ppermute | solution.py:353
  38.2 33.0 %all-to-all-start.1 = ((bf16[32,32,1024]{2,1,0:T(8,128)(2,1)}), bf16[32,32,1024]{2,1,0:T(8,128)(2,1)}, u32[]{:S(2)}, u32[]{:S(2)}) async-start(bf16[32,32,1024]{2,1,0:T(8,128)(2,1)} %bitcast.2), calls=%async_computation.1 | async-start | bytes 4194304 | tf_op jit(solution)/shard_map/all_to_all | solution.py:336
  80.0 32.9 %all-to-all-start.2 = ((bf16[32,32,1024]{2,1,0:T(8,128)(2,1)}), bf16[32,32,1024]{2,1,0:T(8,128)(2,1)S(1)}, u32[]{:S(2)}, u32[]{:S(2)}) async-start(bf16[32,32,1024]{2,1,0:T(8,128)(2,1)} %bitcast.14), calls=%async_computation.2 | async-start | bytes 4194304 | tf_op jit(solution)/shard_map/all_to_all | solution.py:336
  114.4 20.7 %copy-start = (bf16[512,1024]{1,0:T(8,128)(2,1)S(1)}, bf16[512,1024]{1,0:T(8,128)(2,1)}, u32[]{:S(2)}) copy-start(bf16[512,1024]{1,0:T(8,128)(2,1)} %gate_ref.1) | copy-start | bytes 3145732
  114.4 20.7 %copy-start.1 = (f32[1024]{0:T(1024)S(1)}, f32[1024]{0:T(1024)}, u32[]{:S(2)}) copy-start(f32[1024]{0:T(1024)} %param.8) | copy-start | bytes 12292

commit v3 on v2

--- a/solution.py
+++ b/solution.py
@@ -84,16 +84,23 @@
 
 
 def cross_kernel(scale, table_ref, x_ref, o_hbm, o_buf, o_sem):
-    def store(i, cols):
-        return pltpu.make_async_copy(o_buf.at[:, cols], o_hbm.at[:, cols], o_sem.at[i])
+    halves = o_sem.shape[0]
+    half = o_buf.shape[0] // halves
+
+    def store(h, i, cols):
+        rows = pl.ds(h * half, half)
+        return pltpu.make_async_copy(o_buf.at[rows, cols], o_hbm.at[rows, cols], o_sem.at[h, i])
 
     def step(i, cols):
-        acc = jnp.dot(table_ref[...], x_ref[:, cols], preferred_element_type=jnp.float32)
-        o_buf[:, cols] = (acc * scale).astype(o_buf.dtype)
-        store(i, cols).start()
+        for h in range(halves):
+            rows = pl.ds(h * half, half)
+            acc = jnp.dot(table_ref[rows], x_ref[:, cols], preferred_element_type=jnp.float32)
+            o_buf[rows, cols] = (acc * scale).astype(o_buf.dtype)
+            store(h, i, cols).start()
 
     each_block(x_ref.shape[1], step)
-    each_block(x_ref.shape[1], lambda i, cols: store(i, cols).wait())
+    for h in range(halves):
+        each_block(x_ref.shape[1], lambda i, cols, h=h: store(h, i, cols).wait())
 
 
 def fold_kernel(scale, table_ref, x_ref, o_ref):
@@ -245,7 +252,7 @@
 
 def apply_cross(table, x, scale):
     out = jax.ShapeDtypeStruct((table.shape[0], x.shape[1]), jnp.bfloat16)
-    scratch = [pltpu.VMEM(out.shape, out.dtype), pltpu.SemaphoreType.DMA((x.shape[1] // LANES,))]
+    scratch = [pltpu.VMEM(out.shape, out.dtype), pltpu.SemaphoreType.DMA((2, x.shape[1] // LANES))]
     return call(functools.partial(cross_kernel, scale), (), (table, x), out, scratch, 12)
 
 
@@ -293,6 +300,9 @@
         at = pl.ds(i * rows, rows)
         return pltpu.make_async_copy(o_buf.at[at], o_hbm.at[at], o_sem.at[i])
 
+    for i in range(blocks):
+        for load in loads(i):
+            load.start()
     mine = pl.ds(pl.multiple_of(target * width, width), width)
     parts = range(far_buf.shape[0])
     taken = [pltpu.make_async_copy(stored_hbm.at[p, :, mine], far_buf.at[p], far_sem.at[0, p]) for p in parts]
@@ -301,16 +311,13 @@
         copy.start()
     for i in range(blocks):
         for load in loads(i):
-            load.start()
-    for p in parts:
-        taken[p].wait()
-        given[p].start()
-    for i in range(blocks):
-        for load in loads(i):
             load.wait()
         at = slice(i * rows, (i + 1) * rows)
         o_buf[at] = (left[at].astype(jnp.float32) * right[at].astype(jnp.float32)).astype(o_buf.dtype)
         store(i).start()
+    for p in parts:
+        taken[p].wait()
+        given[p].start()
     for i in range(blocks):
         store(i).wait()
     for copy in given:

time: 138 us -> 138 us (level)
  no operation moved by 1% of the time
where the time goes in v3:
time: 138 us; the launch traced here: 137 us
  waiting for transfers between devices  60.8 us (44%)
  starting transfers between devices  23.5 us (17%)
  blocking collectives  20.6 us (15%)
  Pallas kernels  17.8 us (13%)
  other arithmetic  11.2 us (8%)
  local copies, waits for them, and re-layouts  2.81 us (2%)
    all_to_all x3, waiting for transfers between devices, exchange(): return lax.all_to_all(array, 'ctx', split_axis=0, concat_axis=0, tiled=True)  53.8 us
    all_to_all x1, blocking collectives, exchange(): return lax.all_to_all(array, 'ctx', split_axis=0, concat_axis=0, tiled=True)  20.6 us
    all_to_all x3, starting transfers between devices, exchange(): return lax.all_to_all(array, 'ctx', split_axis=0, concat_axis=0, tiled=True)  18.6 us
    pallas_call x4, Pallas kernels, call(): pl.pallas_call(kernel, in_specs=[there] * len(stored) + [pl.BlockSpec(mem...  16.4 us
    ppermute x3, waiting for transfers between devices, send(): lax.ppermute(piece, 'fsdp', [(m, (m + shift) % members) for m in range(me...  7 us
    convert_element_type x2, other arithmetic, local_table(): return jnp.where(keep[None], cosine(step, length), 0.0).astype(jnp.bfloat16)  5.73 us
    ppermute x3, starting transfers between devices, send(): lax.ppermute(piece, 'fsdp', [(m, (m + shift) % members) for m in range(me...  4.91 us
    convert_element_type x2, other arithmetic, cross_table(): jnp.where(same, cosine(step, 2 * devices) * SPREAD, 0.0)  4.83 us
  transfers between devices with their start and end apart: 6, of which 4 were waited for; matrix products, arithmetic and copies ran while one was open for 8% of the time, Pallas kernels for 2%

profile of v3, /device:TPU:1, one launch (start us, length us, event | category | flops | bytes accessed | tf_op | source)
XLA Modules:
  0.0 137.1 jit_solution(7638062079965944528)
XLA Ops:
  0.0 2.8 %shard_map.55 = (bf16[512,1024]{1,0:T(8,128)(2,1)}, bf16[2,256,1024]{2,1,0:T(8,128)(2,1)}) custom-call(bf16[512,1024]{1,0:T(8,128)(2,1)} %left_hbm.1, bf16[512,1024]{1,0:T(8,128)(2,1)} %right_hbm.1, bf16[2,256,4096]{2,1,0:T(8,128)(2,1)} %own_hbm.1), custom_call_target="tpu_custom_call" | custom-call | tf_op jit(solution)/shard_map/pallas_call | solution.py:243
  2.8 2.8 %constant_dynamic-slice_fusion = (bf16[2,256,1024]{2,1,0:T(8,128)(2,1)S(1)}, bf16[2,256,1024]{2,1,0:T(8,128)(2,1)}) fusion(bf16[2,256,4096]{2,1,0:T(8,128)(2,1)} %own_hbm.1, s32[]{:T(128)S(6)} %select_n.443, s32[]{:T(128)S(6)} %select_n.442), kind=kLoop, calls=%fused_computation.126 | loop fusion | bytes 4194312 | tf_op jit(solution)/shard_map/dynamic_slice | solution.py:357
  5.6 2.0 %collective-permute-start = (bf16[2,256,1024]{2,1,0:T(8,128)(2,1)}, bf16[2,256,1024]{2,1,0:T(8,128)(2,1)}, u32[]{:S(2)}, u32[]{:S(2)}) collective-permute-start(bf16[2,256,1024]{2,1,0:T(8,128)(2,1)} %get-tuple-element.16), channel_id=1, source_target_pairs={{0,1},{1,2},{2,3},{3,0},{4,5},{5,6},{6,7},{7,4},{8,9},{9,10},{10,1... | collective-permute-start | bytes 3145736 | tf_op jit(solution)/shard_map/ppermute | solution.py:360
  7.7 1.3 collective-permute-start.2
  8.9 9.5 %all-to-all-start = ((bf16[32,16,1024]{2,1,0:T(8,128)(2,1)}), bf16[32,16,1024]{2,1,0:T(8,128)(2,1)S(1)}, u32[]{:S(2)}, u32[]{:S(2)}) async-start(bf16[32,16,1024]{2,1,0:T(8,128)(2,1)} %bitcast), calls=%async_computation | async-start | bytes 2097152 | tf_op jit(solution)/shard_map/all_to_all | solution.py:343
  18.5 1.6 %collective-permute-start.1 = (bf16[2,256,1024]{2,1,0:T(8,128)(2,1)}, bf16[2,256,1024]{2,1,0:T(8,128)(2,1)}, u32[]{:S(2)}, u32[]{:S(2)}) collective-permute-start(bf16[2,256,1024]{2,1,0:T(8,128)(2,1)} %get-tuple-element.13), channel_id=1, source_target_pairs={{0,2},{1,3},{2,0},{3,1},{4,6},{5,7},{6,4},{7,5},{8,10},{9,11},{10,... | collective-permute-start | bytes 3145736 | tf_op jit(solution)/shard_map/ppermute | solution.py:360
  20.2 0.2 compare_or_fusion
  20.3 2.3 %select_convert_fusion.table_ref = bf16[1024,512]{1,0:T(8,128)(2,1)S(1)} fusion(s32[1024]{0:T(1024)S(1)} %get-tuple-element.17, s32[512]{0:T(512)S(1)} %get-tuple-element.19, s32[1024]{0:T(1024)S(1)} %get-tuple-element.18, s32[512]{0:T(512)S(1)} %get-tuple-element.20, s32[1024]{0:T(1024)S(1)} %fusion.23), kind=kLoop, calls=%fused_computation | loop fusion | flops 14155776 | bytes 1064960 | tf_op jit(solution)/shard_map/convert_element_type | solution.py:48
  22.7 12.7 %all-to-all-done = bf16[32,16,1024]{2,1,0:T(8,128)(2,1)S(1)} async-done(((bf16[32,16,1024]{2,1,0:T(8,128)(2,1)}), bf16[32,16,1024]{2,1,0:T(8,128)(2,1)S(1)}, u32[]{:S(2)}, u32[]{:S(2)}) %all-to-all-start) | async-done | bytes 1048608 | tf_op jit(solution)/shard_map/all_to_all | solution.py:343
  35.4 2.3 %shard_map.56 = bf16[1024,1024]{1,0:T(8,128)(2,1)} custom-call(bf16[1024,512]{1,0:T(8,128)(2,1)S(1)} %select_convert_fusion.table_ref, bf16[512,1024]{1,0:T(8,128)(2,1)S(1)} %bitcast.11), custom_call_target="tpu_custom_call" | custom-call | tf_op jit(solution)/shard_map/pallas_call | solution.py:243
  37.7 4.6 %all-to-all-start.1 = ((bf16[32,32,1024]{2,1,0:T(8,128)(2,1)}), bf16[32,32,1024]{2,1,0:T(8,128)(2,1)}, u32[]{:S(2)}, u32[]{:S(2)}) async-start(bf16[32,32,1024]{2,1,0:T(8,128)(2,1)} %bitcast.2), calls=%async_computation.1 | async-start | bytes 4194304 | tf_op jit(solution)/shard_map/all_to_all | solution.py:343
  42.3 0.2 compare_or_fusion.1
  42.5 0.1 subtract_multiply_fusion
  42.6 0.1 subtract_multiply_fusion.1
  42.7 2.9 %select_convert_fusion.2.m_hbm = bf16[4,512,256]{2,1,0:T(8,128)(2,1)} fusion(s32[512,256]{1,0:T(8,128)S(1)} %subtract_multiply_fusion.1, s32[512]{0:T(512)S(1)} %fusion.37, s32[4,256]{1,0:T(4,128)S(1)} %iota_add_fusion, pred[512,256]{1,0:T(8,128)(4,1)S(1)} %compare_or_fusion.1), kind=kLoop, calls=%fused_computation.18 | loop fusion | flops 13107200 | bytes 1710080 | tf_op jit(solution)/shard_map/convert_element_type | solution.py:75
  45.7 2.8 %select_convert_fusion.1.g_hbm = bf16[4,256,512]{2,1,0:T(8,128)(2,1)} fusion(s32[256,512]{1,0:T(8,128)S(1)} %subtract_multiply_fusion, s32[512]{0:T(512)S(1)} %fusion.37, s32[4,256]{1,0:T(4,128)S(1)} %iota_add_fusion, pred[256,512]{1,0:T(8,128)(4,1)S(1)} %compare_or_fusion), kind=kLoop, calls=%fused_computation.9 | loop fusion | flops 13107200 | bytes 1710080 | tf_op jit(solution)/shard_map/convert_element_type | solution.py:75
  48.5 0.0 collective-permute-done.near_hbm
  48.5 0.0 collective-permute-done.2.last_hbm
  48.5 7.0 %collective-permute-done.1.far_hbm = bf16[2,256,1024]{2,1,0:T(8,128)(2,1)} collective-permute-done((bf16[2,256,1024]{2,1,0:T(8,128)(2,1)}, bf16[2,256,1024]{2,1,0:T(8,128)(2,1)}, u32[]{:S(2)}, u32[]{:S(2)}) %collective-permute-start.1) | collective-permute-done | bytes 1048608 | tf_op jit(solution)/shard_map/ppermute | solution.py:360
  55.5 15.1 %all-to-all-done.1 = bf16[32,32,1024]{2,1,0:T(8,128)(2,1)} async-done(((bf16[32,32,1024]{2,1,0:T(8,128)(2,1)}), bf16[32,32,1024]{2,1,0:T(8,128)(2,1)}, u32[]{:S(2)}, u32[]{:S(2)}) %all-to-all-start.1) | async-done | bytes 2097184 | tf_op jit(solution)/shard_map/all_to_all | solution.py:343
  70.6 8.9 %shard_map.57 = bf16[32,4,8,1024]{3,2,1,0:T(8,128)(2,1)} custom-call(bf16[4,512,256]{2,1,0:T(8,128)(2,1)} %select_convert_fusion.2.m_hbm, bf16[4,256,512]{2,1,0:T(8,128)(2,1)} %select_convert_fusion.1.g_hbm, bf16[2,256,4096]{2,1,0:T(8,128)(2,1)} %own_hbm.1, bf16[2,256,1024]{2,1,0:T(8,128)(2,1)} %collective-permute-done.near_hbm, ...), custom_call_target="tpu_custom_call" | custom-call | tf_op jit(solution)/shard_map/pallas_call | solution.py:243
  79.5 4.5 %all-to-all-start.2 = ((bf16[32,32,1024]{2,1,0:T(8,128)(2,1)}), bf16[32,32,1024]{2,1,0:T(8,128)(2,1)S(1)}, u32[]{:S(2)}, u32[]{:S(2)}) async-start(bf16[32,32,1024]{2,1,0:T(8,128)(2,1)} %bitcast.14), calls=%async_computation.2 | async-start | bytes 4194304 | tf_op jit(solution)/shard_map/all_to_all | solution.py:343
  84.0 2.5 %select_convert_fusion.3.table_ref = bf16[512,1024]{1,0:T(8,128)(2,1)S(1)} fusion(s32[1024]{0:T(1024)S(1)} %get-tuple-element.17, s32[1024]{0:T(1024)S(1)} %get-tuple-element.18, s32[512]{0:T(512)S(1)} %get-tuple-element.19, s32[1024]{0:T(1024)S(1)} %fusion.23, s32[512]{0:T(512)S(1)} %get-tuple-element.20), kind=kLoop, calls=%fused_computation.27 | loop fusion | flops 14155776 | bytes 1064960 | tf_op jit(solution)/shard_map/convert_element_type | solution.py:48
  86.5 25.9 %all-to-all-done.2 = bf16[32,32,1024]{2,1,0:T(8,128)(2,1)S(1)} async-done(((bf16[32,32,1024]{2,1,0:T(8,128)(2,1)}), bf16[32,32,1024]{2,1,0:T(8,128)(2,1)S(1)}, u32[]{:S(2)}, u32[]{:S(2)}) %all-to-all-start.2) | async-done | bytes 2097184 | tf_op jit(solution)/shard_map/all_to_all | solution.py:343
  112.5 1.4 %fold.1 = bf16[512,1024]{1,0:T(8,128)(2,1)S(1)} custom-call(bf16[512,1024]{1,0:T(8,128)(2,1)S(1)} %select_convert_fusion.3.table_ref, bf16[1024,1024]{1,0:T(8,128)(2,1)S(1)} %bitcast.9), custom_call_target="tpu_custom_call" | custom-call | tf_op jit(solution)/shard_map/fold/pallas_call | solution.py:261
  113.9 0.0 copy-start
  113.9 0.0 copy-start.1
  113.9 20.6 %all_to_all.20 = bf16[32,16,1024]{2,1,0:T(8,128)(2,1)S(1)} all-to-all(bf16[32,16,1024]{2,1,0:T(8,128)(2,1)S(1)} %bitcast.12), channel_id=1, replica_groups=mesh['ctx'=32,'fsdp'=4] {'ctx'}, dimensions={0} | all-to-all | bytes 2097152 | tf_op jit(solution)/shard_map/all_to_all | solution.py:343
  134.6 0.0 copy-done
  134.6 0.0 copy-done.1
  134.6 2.4 %shard_map.58 = bf16[512,1024]{1,0:T(8,128)(2,1)} custom-call(bf16[512,1024]{1,0:T(8,128)(2,1)S(1)} %bitcast.10, bf16[512,1024]{1,0:T(8,128)(2,1)} %get-tuple-element.14.mixed_ref, bf16[512,1024]{1,0:T(8,128)(2,1)S(1)} %copy-done, f32[1,1024]{1,0:T(1,128)S(1)} %bitcast.13), custom_call_target="tpu_custom_call" | custom-call | tf_op jit(solution)/shard_map/pallas_call | solution.py:243
  (11 shorter events, 0.1 us)
Async XLA Ops:
  5.6 42.8 %collective-permute-start = (bf16[2,256,1024]{2,1,0:T(8,128)(2,1)}, bf16[2,256,1024]{2,1,0:T(8,128)(2,1)}, u32[]{:S(2)}, u32[]{:S(2)}) collective-permute-start(bf16[2,256,1024]{2,1,0:T(8,128)(2,1)} %get-tuple-element.16), channel_id=1, source_target_pairs={{0,1},{1,2},{2,3},{3,0},{4,5},{5,6},{6,7},{7,4},{8,9},{9,10},{10,1... | collective-permute-start | bytes 3145736 | tf_op jit(solution)/shard_map/ppermute | solution.py:360
  7.7 40.8 %collective-permute-start.2 = (bf16[2,256,1024]{2,1,0:T(8,128)(2,1)S(1)}, bf16[2,256,1024]{2,1,0:T(8,128)(2,1)}, u32[]{:S(2)}, u32[]{:S(2)}) collective-permute-start(bf16[2,256,1024]{2,1,0:T(8,128)(2,1)S(1)} %get-tuple-element.15), channel_id=1, source_target_pairs={{0,3},{1,0},{2,1},{3,2},{4,7},{5,4},{6,5},{7,6},{8,11},{9,8},{10,9... | collective-permute-start | bytes 3145736 | tf_op jit(solution)/shard_map/ppermute | solution.py:360
  8.9 26.4 %all-to-all-start = ((bf16[32,16,1024]{2,1,0:T(8,128)(2,1)}), bf16[32,16,1024]{2,1,0:T(8,128)(2,1)S(1)}, u32[]{:S(2)}, u32[]{:S(2)}) async-start(bf16[32,16,1024]{2,1,0:T(8,128)(2,1)} %bitcast), calls=%async_computation | async-start | bytes 2097152 | tf_op jit(solution)/shard_map/all_to_all | solution.py:343
  18.5 37.0 %collective-permute-start.1 = (bf16[2,256,1024]{2,1,0:T(8,128)(2,1)}, bf16[2,256,1024]{2,1,0:T(8,128)(2,1)}, u32[]{:S(2)}, u32[]{:S(2)}) collective-permute-start(bf16[2,256,1024]{2,1,0:T(8,128)(2,1)} %get-tuple-element.13), channel_id=1, source_target_pairs={{0,2},{1,3},{2,0},{3,1},{4,6},{5,7},{6,4},{7,5},{8,10},{9,11},{10,... | collective-permute-start | bytes 3145736 | tf_op jit(solution)/shard_map/ppermute | solution.py:360
  37.7 32.9 %all-to-all-start.1 = ((bf16[32,32,1024]{2,1,0:T(8,128)(2,1)}), bf16[32,32,1024]{2,1,0:T(8,128)(2,1)}, u32[]{:S(2)}, u32[]{:S(2)}) async-start(bf16[32,32,1024]{2,1,0:T(8,128)(2,1)} %bitcast.2), calls=%async_computation.1 | async-start | bytes 4194304 | tf_op jit(solution)/shard_map/all_to_all | solution.py:343
  79.5 32.9 %all-to-all-start.2 = ((bf16[32,32,1024]{2,1,0:T(8,128)(2,1)}), bf16[32,32,1024]{2,1,0:T(8,128)(2,1)S(1)}, u32[]{:S(2)}, u32[]{:S(2)}) async-start(bf16[32,32,1024]{2,1,0:T(8,128)(2,1)} %bitcast.14), calls=%async_computation.2 | async-start | bytes 4194304 | tf_op jit(solution)/shard_map/all_to_all | solution.py:343
  113.9 20.7 %copy-start = (bf16[512,1024]{1,0:T(8,128)(2,1)S(1)}, bf16[512,1024]{1,0:T(8,128)(2,1)}, u32[]{:S(2)}) copy-start(bf16[512,1024]{1,0:T(8,128)(2,1)} %gate_ref.1) | copy-start | bytes 3145732
  113.9 20.7 %copy-start.1 = (f32[1024]{0:T(1024)S(1)}, f32[1024]{0:T(1024)}, u32[]{:S(2)}) copy-start(f32[1024]{0:T(1024)} %param.8) | copy-start | bytes 12292
